TPU v7x, 256 devices: a whole 4x4x8 slice. The times are simulated.
256 devices in a mesh: gx: 64 (over x, z, core), af: 4 (over y).
Axes of the slice: x: 4, y: 4, z: 8, core: 2. Of those that a mesh axis runs over, the one named last changes fastest.
Arguments:
- scalar_field: float32 [128, 512, 512], P('gx', 'af'), may hold values from -256 to 256
- plane_sketch: float32 [128, 2, 256], P('gx'), may hold values from -0.5 to 0.5
- second_sketch: float32 [512, 256], P('af'), may hold values from -0.25 to 0.25
- third_sketch: float32 [512, 256], replicated, may hold values from -0.25 to 0.25
- mixing: float32 [2, 256, 128], replicated, may hold values from -0.375 to 0.375
- plane_targets: int32 [128, 2], replicated, may hold values from 0 to 7
- plane_signs: int32 [128, 2], replicated, may hold values from 0 to 1
Outputs:
- factor_second: float32 [512, 128], P(('af', 'gx'))
- factor_third: float32 [512, 128], P(('gx', 'af'))
- core_sketch: float32 [128, 128, 128], P('gx', 'af')
Inputs may be any that keep to these rules, and one draw needn't show every extreme that they name: `plane_targets`: block id of each of a plane's two entries in the core sketch; the two may coincide. `plane_signs`: 1 stands for a plus sign, 0 for a minus sign.
All inputs are finite; a program needn't handle non-finite values.
Results may differ from a plain program's by a relative error of at most 0.0003.
Values sent between devices are 32-bit elements; how exact they have to be, the bound alone decides.
A program may use at most 64 MiB of HBM per device.

v0:
```python
import jax
import jax.numpy as jnp
from jax import lax
from jax.sharding import PartitionSpec as P

BLOCK = 16
BLOCKS = 8
precise = lax.Precision.HIGHEST


def gram_of(ranged):
    return jnp.dot(ranged.T, ranged, precision=precise)


def orthonormal_rows(ranged, gram_matrix):
    lower_factor = jnp.linalg.cholesky(gram_matrix)
    return jax.scipy.linalg.solve_triangular(lower_factor, ranged.T, lower=True).T


def selector(targets, sign_values, row_count):
    row_ids = jnp.arange(row_count, dtype=jnp.int32)
    return jnp.sum(
        jnp.where(targets[None, :, :] == row_ids[:, None, None], sign_values[None, :, :], 0.0),
        axis=2,
    )


def body(
    scalar_field, plane_sketch, second_sketch, third_sketch, mixing, plane_targets, plane_signs
):
    planes, rows, cells = scalar_field.shape
    rank_cols = mixing.shape[2]
    gx_index = lax.axis_index("gx")
    af_index = lax.axis_index("af")
    gx_size = lax.axis_size("gx")
    af_size = lax.axis_size("af")
    along_second = jnp.einsum("pjl,lk->pjk", scalar_field, third_sketch, precision=precise)
    partial_second = jnp.einsum(
        "pjk,pk->jk", along_second, plane_sketch[:, 0, :], precision=precise
    )
    along_third = jnp.einsum("pjl,jk->plk", scalar_field, second_sketch, precision=precise)
    partial_third = jnp.einsum("plk,pk->lk", along_third, plane_sketch[:, 1, :], precision=precise)
    range_second_block = jnp.dot(partial_second, mixing[0], precision=precise)
    range_third = jnp.dot(partial_third, mixing[1], precision=precise)
    full_rows = rows * af_size
    range_second = lax.dynamic_update_slice_in_dim(
        jnp.zeros((full_rows, rank_cols), jnp.float32), range_second_block, af_index * rows, 0
    )
    both = lax.psum(jnp.stack([range_second, range_third]), ("gx", "af"))
    rows_second, rows_third = (both[0], both[1])
    factor_second_all = orthonormal_rows(rows_second, gram_of(rows_second))
    factor_third_all = orthonormal_rows(rows_third, gram_of(rows_third))
    out_second = full_rows // (gx_size * af_size)
    factor_second = lax.dynamic_slice_in_dim(
        factor_second_all, (af_index * gx_size + gx_index) * out_second, out_second, 0
    )
    factor_third = lax.dynamic_slice_in_dim(
        factor_third_all, (gx_index * af_size + af_index) * out_second, out_second, 0
    )
    basis_second = lax.dynamic_slice_in_dim(factor_second_all, af_index * rows, rows, 0)
    left_side = jnp.einsum("jr,pjl->prl", basis_second, scalar_field, precision=precise)
    projected = jnp.einsum("prl,ls->prs", left_side, factor_third_all, precision=precise)
    out_rows = BLOCKS * BLOCK // gx_size
    plane_ids = jnp.arange(plane_targets.shape[0], dtype=jnp.int32)
    all_targets = plane_targets * BLOCK + (plane_ids % BLOCK)[:, None]
    all_signs = (2 * plane_signs - 1).astype(jnp.float32)
    first_plane = gx_index * planes
    own_targets = lax.dynamic_slice_in_dim(all_targets, first_plane, planes, 0)
    own_signs = lax.dynamic_slice_in_dim(all_signs, first_plane, planes, 0)
    flattened = projected.reshape(planes, -1)
    select = selector(own_targets, own_signs, gx_size * out_rows)
    partial_core = lax.psum_scatter(
        jnp.dot(select, flattened, precision=precise).reshape(
            gx_size * out_rows, rank_cols, rank_cols
        ),
        "gx",
        scatter_dimension=0,
        tiled=True,
    )
    core_sketch = lax.psum_scatter(partial_core, "af", scatter_dimension=1, tiled=True)
    return (factor_second, factor_third, core_sketch)


def solution(mesh):
    in_specs = (P("gx", "af", None), P("gx", None, None), P("af", None), P(), P(), P(), P())
    out_specs = (P(("af", "gx"), None), P(("gx", "af"), None), P("gx", "af", None))
    return jax.shard_map(body, mesh=mesh, in_specs=in_specs, out_specs=out_specs, check_vma=False)
```

profile of v0, /device:TPU:2, one launch (start us, length us, event | category | flops | bytes accessed | tf_op | source)
XLA Modules:
  0.0 544.3 jit_solution(9497696338969925887)
XLA Ops:
  7.2 0.0 copy-start
  7.2 0.0 all-reduce.4.cloned.1.call-start
  7.2 0.8 fusion.37
  8.0 0.2 copy-done
  8.2 2.0 fusion.1
  10.2 1.5 convolution_bitcast_fusion.2
  11.7 1.6 fusion.3
  13.4 1.2 fusion.4
  14.6 0.8 pad_maximum_fusion
  15.4 0.0 all-reduce.4.cloned.1.call-update
  15.4 0.2 reduce-scatter.2.cloned.1.call-start
  15.7 0.7 add_convert_fusion
  16.4 0.7 multiply_add_fusion
  17.1 0.1 constant_dynamic-slice_fusion
  17.1 0.1 copy.38
  17.2 0.1 constant_dynamic-slice_fusion.1
  17.3 0.1 copy.37
  17.4 0.1 fusion.34
  17.5 253.1 %all-reduce.4.cloned.1.call-done = f32[2,512,128]{2,1,0:T(8,128)} async-done(((f32[2,512,128]{2,1,0:T(8,128)}), f32[2,512,128]{2,1,0:T(8,128)}) %all-reduce.4.cloned.1.call-update) | async-done | bytes 524304 | tf_op jit(solution)/shard_map/psum | solution.py:49
  270.6 1.6 fusion.13
  272.2 0.1 copy.35
  272.3 11.7 %cholesky.44 = f32[128,128]{1,0:T(8,128)S(1)} custom-call(f32[128,128]{1,0:T(8,128)S(1)} %fusion.32), custom_call_target="Cholesky" | custom-call | tf_op jit(solution)/shard_map/jit(cholesky)/cholesky | solution.py:16
  284.0 0.6 compare_reduce_fusion.1
  284.7 0.7 fusion.26
  285.4 9.8 %custom-call.6 = f32[1,128,128]{1,2,0:T(8,128)S(1)} custom-call(f32[1,128,128]{2,1,0:T(8,128)S(1)} %fusion.26), custom_call_target="InvertDiagBlocksLowerTriangular" | custom-call | tf_op jit(solution)/shard_map/jit(_solve_triangular)/triangular_solve | solution.py:17
  295.2 1.6 fusion.11
  296.8 0.1 copy.36
  296.9 11.7 %cholesky.55 = f32[128,128]{1,0:T(8,128)S(1)} custom-call(f32[128,128]{1,0:T(8,128)S(1)} %fusion.30), custom_call_target="Cholesky" | custom-call | tf_op jit(solution)/shard_map/jit(cholesky)/cholesky | solution.py:16
  308.7 0.6 compare_reduce_fusion
  309.3 0.7 fusion.27
  310.0 10.0 %custom-call.7 = f32[1,128,128]{1,2,0:T(8,128)S(1)} custom-call(f32[1,128,128]{2,1,0:T(8,128)S(1)} %fusion.27), custom_call_target="InvertDiagBlocksLowerTriangular" | custom-call | tf_op jit(solution)/shard_map/jit(_solve_triangular)/triangular_solve | solution.py:17
  320.0 1.4 fusion.8
  321.3 0.6 convolution_bitcast_fusion.1
  321.9 1.4 fusion.6
  323.3 0.6 convolution_bitcast_fusion.4
  323.9 6.8 %fusion.19 = f32[128,128,128]{2,0,1:T(8,128)S(1)} fusion(f32[1,2,128,128]{3,2,1,0:T(8,128)S(1)} %convolution_bitcast_fusion.4, f32[128,2]{0,1:T(2,128)S(1)} %fusion.34), kind=kOutput, calls=%fused_computation.27 | convolution fusion | flops 50331648 | bytes 8520704 | tf_op jit(solution)/shard_map/dot_general | solution.py:73
  330.7 8.3 %copy.39 = f32[128,128,128]{2,1,0:T(8,128)} copy(f32[128,128,128]{2,0,1:T(8,128)S(1)} %fusion.19) | data formatting | bytes 16777216 | tf_op jit(solution)/shard_map/dot_general | solution.py:73
  339.0 0.0 copy-start.1
  339.0 0.0 reduce-scatter.2.cloned.1.call-update
  339.0 0.0 all-reduce.6.cloned.1.call-start
  339.1 0.6 copy-done.1
  339.7 0.6 dynamic-slice.12
  340.9 147.6 %reduce-scatter.2.cloned.1.call-done = f32[2,128,128]{2,1,0:T(8,128)} async-done(((f32[128,128,128]{2,1,0:T(8,128)}), f32[2,128,128]{2,1,0:T(8,128)}) %reduce-scatter.2.cloned.1.call-update) | async-done | bytes 131088 | tf_op jit(solution)/shard_map/reduce_scatter | solution.py:72
  488.6 1.6 copy.40
  490.2 0.0 all-reduce.6.cloned.1.call-update
  490.2 0.1 dynamic-slice_bitcast_fusion.1
  490.3 0.6 copy.41
  490.9 0.1 dynamic-slice_bitcast_fusion
  491.0 0.6 copy.42
  491.7 44.7 %all-reduce.6.cloned.1.call-done = f32[2,128,128]{2,0,1:T(2,128)} async-done(((f32[2,128,128]{2,0,1:T(2,128)}), f32[2,128,128]{2,0,1:T(2,128)}) %all-reduce.6.cloned.1.call-update) | async-done | bytes 131088
  536.4 0.8 constant_dynamic-slice_fusion.2
  537.1 0.6 copy.43
  (7 shorter events, 0.1 us)
Async XLA Ops:
  7.2 1.1 copy-start
  7.2 263.4 %all-reduce.4.cloned.1.call-start = ((), (), s32[]{:S(2)}) async-start(), calls=%async_computation.1 | async-start | bytes 1048576 | tf_op jit(solution)/shard_map/psum | solution.py:49
  15.4 473.1 %reduce-scatter.2.cloned.1.call-start = ((), (), s32[]{:S(2)}) async-start(), calls=%async_computation.2 | async-start | bytes 8519680 | tf_op jit(solution)/shard_map/reduce_scatter | solution.py:72
  339.0 0.7 copy-start.1
  339.0 197.4 %all-reduce.6.cloned.1.call-start = ((), (), s32[]{:S(2)}) async-start(), calls=%async_computation.3 | async-start | bytes 262144
Sparse Core Ops, SparseCore 0:
  15.6 254.9 all-reduce.3
  339.1 149.3 reduce-scatter.1
  491.0 45.3 all-reduce.5
where the time goes:
time: 545 us; the launch traced here: 544 us
  waiting for transfers between devices  445 us (82%)
  other arithmetic  48.2 us (9%)
  matrix products  20.2 us (4%)
  local copies, waits for them, and re-layouts  15.5 us (3%)
  between operations  14.6 us (3%)
    psum x1, waiting for transfers between devices, body(): both = lax.psum(jnp.stack([range_second, range_third]), ('gx', 'af'))  253 us
    reduce_scatter x1, waiting for transfers between devices, body(): lax.psum_scatter(jnp.dot(select, flattened, precision=precise).reshape(gx...  148 us
    unnamed x4, waiting for transfers between devices  44.8 us
    another operation x6, other arithmetic, orthonormal_rows(): lower_factor = jnp.linalg.cholesky(gram_matrix)  24.8 us
    another operation x4, other arithmetic, orthonormal_rows(): jax.scipy.linalg.solve_triangular(lower_factor, ranged.T, lower=True)  21.1 us
  transfers between devices with their start and end apart: 3, of which 3 were waited for; matrix products, arithmetic and copies ran while one was open for 1% of the time, Pallas kernels for 0%

commit v1 on v0

--- a/solution.py
+++ b/solution.py
@@ -46,7 +46,9 @@
     range_second = lax.dynamic_update_slice_in_dim(
         jnp.zeros((full_rows, rank_cols), jnp.float32), range_second_block, af_index * rows, 0
     )
-    both = lax.psum(jnp.stack([range_second, range_third]), ("gx", "af"))
+    both = jnp.stack([range_second, range_third])
+    for name in ("af", "gx"):
+        both = lax.psum(both, name)
     rows_second, rows_third = (both[0], both[1])
     factor_second_all = orthonormal_rows(rows_second, gram_of(rows_second))
     factor_third_all = orthonormal_rows(rows_third, gram_of(rows_third))

time: 545 us -> 524 us (0.961)
  waiting for transfers between devices: 445 us -> 425 us
    psum x1 -> x2, waiting for transfers between devices: 253 us -> 234 us  [body(): both = lax.psum(both, name)]
    unnamed x4 -> x5, waiting for transfers between devices: 44.8 us -> 44.6 us
  transfers between devices with their start and end apart: 3 -> 4, of which waited for: 3 -> 4; matrix products, arithmetic and copies ran while one was open for 1% -> 1% of each run, Pallas kernels for 0% -> 0%
where the time goes in v1:
time: 524 us
  waiting for transfers between devices  425 us (81%)
  other arithmetic  48.2 us (9%)
  matrix products  20.2 us (4%)
  local copies, waits for them, and re-layouts  15.5 us (3%)
  between operations  14.6 us (3%)
    psum x2, waiting for transfers between devices, body(): both = lax.psum(both, name)  234 us
    reduce_scatter x1, waiting for transfers between devices, body(): lax.psum_scatter(jnp.dot(select, flattened, precision=precise).reshape(gx...  146 us
    unnamed x5, waiting for transfers between devices  44.6 us
    another operation x6, other arithmetic, orthonormal_rows(): lower_factor = jnp.linalg.cholesky(gram_matrix)  24.8 us
    another operation x4, other arithmetic, orthonormal_rows(): jax.scipy.linalg.solve_triangular(lower_factor, ranged.T, lower=True)  21.1 us
  transfers between devices with their start and end apart: 4, of which 4 were waited for; matrix products, arithmetic and copies ran while one was open for 1% of the time, Pallas kernels for 0%

profile of v1, /device:TPU:2, one launch (start us, length us, event | category | flops | bytes accessed | tf_op | source)
XLA Modules:
  0.0 523.7 jit_solution(240091031834976698)
XLA Ops:
  7.2 0.0 copy-start
  7.2 0.0 all-reduce.5.cloned.1.call-start
  7.2 0.8 fusion.37
  8.0 0.2 copy-done
  8.2 2.0 fusion.1
  10.2 1.5 convolution_bitcast_fusion.2
  11.7 1.6 fusion.3
  13.4 1.2 fusion.4
  14.6 0.8 pad_maximum_fusion
  15.4 0.0 all-reduce.5.cloned.1.call-update
  15.4 0.0 all-reduce.7.cloned.1.call-start
  15.5 0.7 add_convert_fusion
  16.2 0.7 multiply_add_fusion
  16.9 49.8 %all-reduce.5.cloned.1.call-done = f32[2,512,128]{2,1,0:T(8,128)} async-done(((f32[2,512,128]{2,1,0:T(8,128)}), f32[2,512,128]{2,1,0:T(8,128)}) %all-reduce.5.cloned.1.call-update) | async-done | bytes 524304 | tf_op jit(solution)/shard_map/psum | solution.py:51
  66.7 0.0 all-reduce.7.cloned.1.call-update
  66.7 0.2 reduce-scatter.2.cloned.1.call-start
  66.9 0.1 constant_dynamic-slice_fusion
  67.0 0.1 copy.38
  67.1 0.1 constant_dynamic-slice_fusion.1
  67.2 0.1 copy.37
  67.3 0.1 fusion.34
  67.4 184.5 %all-reduce.7.cloned.1.call-done = f32[2,512,128]{2,1,0:T(8,128)} async-done(((f32[2,512,128]{2,1,0:T(8,128)}), f32[2,512,128]{2,1,0:T(8,128)}) %all-reduce.7.cloned.1.call-update) | async-done | bytes 524304 | tf_op jit(solution)/shard_map/psum | solution.py:51
  251.9 1.6 fusion.13
  253.5 0.1 copy.35
  253.7 11.7 %cholesky.44 = f32[128,128]{1,0:T(8,128)S(1)} custom-call(f32[128,128]{1,0:T(8,128)S(1)} %fusion.32), custom_call_target="Cholesky" | custom-call | tf_op jit(solution)/shard_map/jit(cholesky)/cholesky | solution.py:16
  265.4 0.6 compare_reduce_fusion.1
  266.0 0.7 fusion.26
  266.7 9.8 %custom-call.6 = f32[1,128,128]{1,2,0:T(8,128)S(1)} custom-call(f32[1,128,128]{2,1,0:T(8,128)S(1)} %fusion.26), custom_call_target="InvertDiagBlocksLowerTriangular" | custom-call | tf_op jit(solution)/shard_map/jit(_solve_triangular)/triangular_solve | solution.py:17
  276.5 1.6 fusion.11
  278.1 0.1 copy.36
  278.3 11.7 %cholesky.55 = f32[128,128]{1,0:T(8,128)S(1)} custom-call(f32[128,128]{1,0:T(8,128)S(1)} %fusion.30), custom_call_target="Cholesky" | custom-call | tf_op jit(solution)/shard_map/jit(cholesky)/cholesky | solution.py:16
  290.0 0.6 compare_reduce_fusion
  290.7 0.7 fusion.27
  291.3 10.0 %custom-call.7 = f32[1,128,128]{1,2,0:T(8,128)S(1)} custom-call(f32[1,128,128]{2,1,0:T(8,128)S(1)} %fusion.27), custom_call_target="InvertDiagBlocksLowerTriangular" | custom-call | tf_op jit(solution)/shard_map/jit(_solve_triangular)/triangular_solve | solution.py:17
  301.3 1.4 fusion.8
  302.7 0.6 convolution_bitcast_fusion.1
  303.3 1.4 fusion.6
  304.6 0.6 convolution_bitcast_fusion.4
  305.2 6.8 %fusion.19 = f32[128,128,128]{2,0,1:T(8,128)S(1)} fusion(f32[1,2,128,128]{3,2,1,0:T(8,128)S(1)} %convolution_bitcast_fusion.4, f32[128,2]{0,1:T(2,128)S(1)} %fusion.34), kind=kOutput, calls=%fused_computation.27 | convolution fusion | flops 50331648 | bytes 8520704 | tf_op jit(solution)/shard_map/dot_general | solution.py:75
  312.0 8.3 %copy.39 = f32[128,128,128]{2,1,0:T(8,128)} copy(f32[128,128,128]{2,0,1:T(8,128)S(1)} %fusion.19) | data formatting | bytes 16777216 | tf_op jit(solution)/shard_map/dot_general | solution.py:75
  320.3 0.0 copy-start.1
  320.3 0.0 reduce-scatter.2.cloned.1.call-update
  320.4 0.0 all-reduce.9.cloned.1.call-start
  320.4 0.6 copy-done.1
  321.0 0.6 dynamic-slice.12
  322.3 145.9 %reduce-scatter.2.cloned.1.call-done = f32[2,128,128]{2,1,0:T(8,128)} async-done(((f32[128,128,128]{2,1,0:T(8,128)}), f32[2,128,128]{2,1,0:T(8,128)}) %reduce-scatter.2.cloned.1.call-update) | async-done | bytes 131088 | tf_op jit(solution)/shard_map/reduce_scatter | solution.py:74
  468.1 1.6 copy.40
  469.8 0.0 all-reduce.9.cloned.1.call-update
  469.8 0.1 dynamic-slice_bitcast_fusion.1
  469.9 0.6 copy.41
  470.6 0.1 dynamic-slice_bitcast_fusion
  470.6 0.6 copy.42
  471.3 44.5 %all-reduce.9.cloned.1.call-done = f32[2,128,128]{2,0,1:T(2,128)} async-done(((f32[2,128,128]{2,0,1:T(2,128)}), f32[2,128,128]{2,0,1:T(2,128)}) %all-reduce.9.cloned.1.call-update) | async-done | bytes 131088
  515.8 0.8 constant_dynamic-slice_fusion.2
  516.6 0.6 copy.43
  (7 shorter events, 0.1 us)
Async XLA Ops:
  7.2 1.1 copy-start
  7.2 59.5 %all-reduce.5.cloned.1.call-start = ((), (), s32[]{:S(2)}) async-start(), calls=%async_computation.1 | async-start | bytes 1048576 | tf_op jit(solution)/shard_map/psum | solution.py:51
  15.4 236.5 %all-reduce.7.cloned.1.call-start = ((), (), s32[]{:S(2)}) async-start(), calls=%async_computation.2 | async-start | bytes 1048576 | tf_op jit(solution)/shard_map/psum | solution.py:51
  66.7 401.4 %reduce-scatter.2.cloned.1.call-start = ((), (), s32[]{:S(2)}) async-start(), calls=%async_computation.3 | async-start | bytes 8519680 | tf_op jit(solution)/shard_map/reduce_scatter | solution.py:74
  320.3 0.7 copy-start.1
  320.4 195.5 %all-reduce.9.cloned.1.call-start = ((), (), s32[]{:S(2)}) async-start(), calls=%async_computation.4 | async-start | bytes 262144
Sparse Core Ops, SparseCore 0:
  15.6 51.0 all-reduce.4
  70.2 181.6 all-reduce.6
  320.5 147.6 reduce-scatter.1
  470.4 45.3 all-reduce.8
